TPU v7x, 128 devices: a whole 4x4x4 slice. The times are simulated.
128 devices in a mesh: head: 4 (over y), tok: 32 (over x, z, core).
Axes of the slice: x: 4, y: 4, z: 4, core: 2. Of those that a mesh axis runs over, the one named last changes fastest.
Arguments:
- tokens: bfloat16 [8192, 2048], P(('tok', 'head')), may hold values from -6 to 6
- token_req: int32 [8192], P(('tok', 'head')), may hold values from 0 to 1, as said below
- cache_len: int32 [64], P('tok'), may hold values from 16 to 1023, as said below
- sink_count: int32 [64], P('tok'), may hold values from 1 to 8
- cache_k: bfloat16 [64, 1024, 2048], P('tok', None, 'head'), may hold values from -64 to 64
- cache_v: bfloat16 [64, 1024, 2048], P('tok', None, 'head'), may hold values from -6 to 6
- attn_gain: float32 [2048], replicated, may hold values from 0.1 to 1.9
- w_qkv: bfloat16 [2048, 3, 2048], P(None, None, 'head'), may hold values from -0.125 to 0.125
- w_out: bfloat16 [2048, 2048], P('head'), may hold values from -0.125 to 0.125
- ffn_gain: float32 [2048], replicated, may hold values from 0.1 to 1.9
- routes: int32 [8192, 8], P(('tok', 'head')), may hold values from 0 to 63, all different within a row; in each aligned block of 64 rows (0 to 63, 64 to 127, ...) at most 16 rows name the same one
- route_weight: float32 [8192, 8], P(('tok', 'head')), may hold values from 0.1 to 1
- w_expert: bfloat16 [64, 3, 2048, 1024], P('tok', None, None, 'head'), may hold values from -0.125 to 0.125
Outputs:
- hidden_out: bfloat16 [8192, 2048], P(('tok', 'head'))
- new_cache_k: bfloat16 [64, 1024, 2048], P('tok', None, 'head')
- new_cache_v: bfloat16 [64, 1024, 2048], P('tok', None, 'head')
Inputs may be any that keep to these rules, and one draw needn't show every extreme that they name: `token_req`: within each group of 256 consecutive tokens, the tokens of request 0 come first and those of request 1 follow; each request has at least one token. `cache_len`: A request's cache length plus its number of tokens is at most 1024. `routes`: each row names 8 different experts; in each aligned block of 64 rows (the rows of one device) no expert is named more than 16 times.
All inputs are finite; a program needn't handle non-finite values.
Results may differ from a plain program's by a relative error of at most 0.018.
Values may be sent and summed in bfloat16 or wider, within the bound.
No kernel may reach another device: no remote copies, remote signals or barrier semaphores. Data moves between devices by JAX's collectives and lax.ppermute only.
A program may use at most 192 MiB of HBM per device.

v0:
```python
import jax
import jax.numpy as jnp
from jax import lax
from jax.sharding import PartitionSpec as P

HD = 128
REQ_GRP = 2
CAP = 1024
WIN = 384
norm_eps = 1e-05
rope_base = 50000.0


def rms_norm(values, gain_vec):
    widened = values.astype(jnp.float32)
    return (
        widened
        * lax.rsqrt(jnp.mean(widened * widened, axis=-1, keepdims=True) + norm_eps)
        * gain_vec
    )


def rotate(vectors, positions_all):
    half_width = vectors.shape[-1] // 2
    frequency = rope_base ** (
        -(jnp.arange(half_width, dtype=jnp.float32) * 2.0 / vectors.shape[-1])
    )
    angles = positions_all.astype(jnp.float32)[:, None] * frequency[None, :]
    cosine = jnp.cos(angles)[:, None, :]
    sine_part = jnp.sin(angles)[:, None, :]
    first_half = vectors[..., :half_width]
    second_half = vectors[..., half_width:]
    return jnp.concatenate(
        [
            first_half * cosine - second_half * sine_part,
            second_half * cosine + first_half * sine_part,
        ],
        axis=-1,
    )


def positions(request, lengths):
    one_hot = (request[:, None] == jnp.arange(REQ_GRP, dtype=jnp.int32)[None, :]).astype(jnp.int32)
    before = jnp.cumsum(one_hot, axis=0) - one_hot
    return jnp.sum(one_hot * (before + lengths[None, :]), axis=1)


def attend(query, keys_all, values_all, request, positions_all, sink_counts):
    scores = jnp.einsum(
        "thd,rjhd->thrj", query, keys_all, preferred_element_type=jnp.float32
    ) * HD ** (-0.5)
    slot_ids = jnp.arange(CAP, dtype=jnp.int32)
    same_req = jnp.arange(REQ_GRP, dtype=jnp.int32)[None, :, None] == request[:, None, None]
    causal = slot_ids[None, None, :] <= positions_all[:, None, None]
    window = (slot_ids[None, None, :] < sink_counts[None, :, None]) | (
        slot_ids[None, None, :] > positions_all[:, None, None] - WIN
    )
    allowed = (same_req & causal & window)[:, None]
    masked = jnp.where(allowed, scores, -1e30)
    row_max = jnp.max(masked, axis=(2, 3), keepdims=True)
    exp_scores = jnp.exp(masked - row_max)
    weights = (exp_scores / jnp.sum(exp_scores, axis=(2, 3), keepdims=True)).astype(jnp.bfloat16)
    return jnp.einsum(
        "thrj,rjhd->thd", weights, values_all, preferred_element_type=jnp.float32
    ).astype(jnp.bfloat16)


def expert_apply(slot_rows, weight_set):
    gate_part = jnp.einsum(
        "semd,edf->semf", slot_rows, weight_set[:, 0], preferred_element_type=jnp.float32
    )
    up_part = jnp.einsum(
        "semd,edf->semf", slot_rows, weight_set[:, 1], preferred_element_type=jnp.float32
    )
    hidden = (jax.nn.silu(gate_part) * up_part).astype(jnp.bfloat16)
    return jnp.einsum(
        "semf,edf->semd", hidden, weight_set[:, 2], preferred_element_type=jnp.float32
    )


def on_device(
    tokens,
    token_req,
    cache_len,
    sink_count,
    cache_k,
    cache_v,
    attn_gain,
    w_qkv,
    w_out,
    ffn_gain,
    routes,
    route_weight,
    w_expert,
):
    tok_dev, model_width = tokens.shape
    heads_here = w_qkv.shape[2] // HD
    tok_count = lax.axis_size("tok")
    normed = rms_norm(tokens, attn_gain).astype(jnp.bfloat16)
    group_rows, group_req = (
        lax.all_gather(normed, "head", axis=0, tiled=True),
        lax.all_gather(token_req, "head", axis=0, tiled=True),
    )
    rows_all = group_rows.shape[0]
    positions_all = positions(group_req, cache_len)
    projected = jnp.dot(
        group_rows,
        w_qkv.reshape(model_width, 3 * heads_here * HD),
        preferred_element_type=jnp.float32,
    )
    projected = projected.reshape(rows_all, 3, heads_here, HD)
    query = rotate(projected[:, 0], positions_all).astype(jnp.bfloat16)
    key_new = (
        rotate(projected[:, 1], positions_all)
        .astype(jnp.bfloat16)
        .reshape(rows_all, heads_here * HD)
    )
    value_new = projected[:, 2].astype(jnp.bfloat16).reshape(rows_all, heads_here * HD)
    cache_keys = cache_k.at[group_req, positions_all].set(key_new)
    cache_values = cache_v.at[group_req, positions_all].set(value_new)
    attended = attend(
        query,
        cache_keys.reshape(REQ_GRP, CAP, heads_here, HD),
        cache_values.reshape(REQ_GRP, CAP, heads_here, HD),
        group_req,
        positions_all,
        sink_count,
    )
    attended = attended.reshape(rows_all, heads_here * HD)
    mixed_attn = lax.psum_scatter(
        jnp.dot(attended, w_out, preferred_element_type=jnp.float32).astype(jnp.bfloat16),
        "head",
        scatter_dimension=0,
        tiled=True,
    ).astype(jnp.float32)
    residual = (tokens.astype(jnp.float32) + mixed_attn).astype(jnp.bfloat16)
    ffn_input = rms_norm(residual, ffn_gain).astype(jnp.bfloat16)
    route_count = routes.shape[1]
    exp_dev = w_expert.shape[0]
    expert_total = exp_dev * tok_count
    slot_depth = 2 * tok_dev * route_count // expert_total
    flat_expert = routes.reshape(-1)
    one_hot = (flat_expert[:, None] == jnp.arange(expert_total, dtype=jnp.int32)[None, :]).astype(
        jnp.int32
    )
    before = jnp.cumsum(one_hot, axis=0) - one_hot
    slot_index = jnp.sum(before * one_hot, axis=1)
    target = flat_expert * slot_depth + slot_index
    dispatch = (
        jnp.arange(expert_total * slot_depth, dtype=jnp.int32)[:, None] == target[None, :]
    ).astype(jnp.bfloat16)
    repeated = jnp.repeat(ffn_input, route_count, axis=0)
    outgoing = jnp.dot(dispatch, repeated, preferred_element_type=jnp.float32).astype(jnp.bfloat16)
    outgoing = outgoing.reshape(tok_count, exp_dev, slot_depth, model_width)
    arrived = lax.all_to_all(outgoing, "tok", split_axis=0, concat_axis=0, tiled=True)
    result = expert_apply(arrived, lax.all_gather(w_expert, "head", axis=3, tiled=True)).astype(
        jnp.bfloat16
    )
    returned = lax.all_to_all(result, "tok", split_axis=0, concat_axis=0, tiled=True)
    picked = returned.reshape(-1, model_width)[target].reshape(tok_dev, route_count, model_width)
    combined = jnp.sum(route_weight[:, :, None] * picked.astype(jnp.float32), axis=1)
    hidden_out = (residual.astype(jnp.float32) + combined).astype(jnp.bfloat16)
    return (hidden_out, cache_keys, cache_values)


def solution(mesh):
    return jax.shard_map(
        on_device,
        mesh=mesh,
        in_specs=(
            P(("tok", "head"), None),
            P(("tok", "head")),
            P("tok"),
            P("tok"),
            P("tok", None, "head"),
            P("tok", None, "head"),
            P(),
            P(None, None, "head"),
            P("head", None),
            P(),
            P(("tok", "head"), None),
            P(("tok", "head"), None),
            P("tok", None, None, "head"),
        ),
        out_specs=(P(("tok", "head"), None), P("tok", None, "head"), P("tok", None, "head")),
        check_vma=False,
    )
```

profile of v0, /device:TPU:1, one launch (start us, length us, event | category | flops | bytes accessed | tf_op | source)
XLA Modules:
  0.0 493.8 jit_solution(6323877021367566477)
XLA Ops:
  7.2 0.0 copy-start
  7.2 0.0 all-gather.3.cloned.1.call-start
  7.3 3.2 copy.96
  10.5 1.3 copy.97
  11.8 0.2 fusion.31
  12.0 0.8 fusion.33
  12.8 0.0 all-gather.3.cloned.1.call-update
  12.8 0.0 reduce-scatter.2.cloned.1.call-start
  12.9 0.7 dynamic-slice
  14.3 0.2 dynamic-update-slice
  14.5 7.8 %all-reduce = s32[256]{0:T(256)S(1)} all-reduce(s32[256]{0:T(256)S(1)} %dynamic-update-slice), channel_id=1, replica_groups=mesh['head'=4,'tok'=32] {'head'}, use_global_device_ids=true, to_apply=%add | all-reduce | flops 256 | bytes 2048
  22.4 0.6 reduce-window.14
  23.0 0.2 slice_reduce_fusion.1
  23.2 0.2 reduce-window.15
  23.4 0.1 add_bitcast_fusion.1
  23.5 8.9 %copy.40 = bf16[2048,3,512]{0,2,1:T(8,128)(2,1)} copy(bf16[2048,3,512]{2,0,1:T(8,128)(2,1)} %param.20) | data formatting | bytes 12582912 | tf_op args[7]
  32.4 0.1 fusion.48
  32.5 0.1 iota_compare_fusion.6
  32.6 0.3 multiply_cosine_fusion
  32.9 0.3 iota_compare_fusion.2
  33.2 0.6 or_and_fusion
  33.8 4.4 all-gather.3.cloned.1.call-done
  38.2 5.0 %fusion.27 = f32[256,3,4,128]{0,3,2,1:T(8,128)S(1)} fusion(bf16[3,4,128,2048]{3,2,1,0:T(8,128)(2,1)} %bitcast.168, bf16[256,2048]{1,0:T(8,128)(2,1)} %all-gather.3.cloned.1.call-done), kind=kOutput, calls=%fused_computation.39 | convolution fusion | flops 1610612736 | bytes 8912896 | tf_op jit(solution)/shard_map/dot_general | solution.py:106
  43.2 0.1 slice_bitcast_fusion.10
  43.4 0.7 slice.98
  44.1 0.8 subtract_convert_fusion
  44.9 0.1 copy.42
  45.0 1.1 copy.41
  46.1 34.8 %scatter_fusion.1 = bf16[2,1024,512]{2,1,0:T(8,128)(2,1)} fusion(bf16[2,1024,512]{2,1,0:T(8,128)(2,1)} %copy.96, s32[256]{0:T(256)S(1)} %bitcast.166, bf16[256,512]{1,0:T(8,128)(2,1)S(1)} %copy.42), kind=kCustom, calls=%fused_computation.2 | custom fusion | bytes 788480 | tf_op jit(solution)/shard_map/scatter | solution.py:119
  80.9 3.1 fusion.4
  84.0 3.2 copy-done.2
  87.2 1.8 fusion.3
  89.0 34.6 %scatter_fusion = bf16[2,1024,512]{2,1,0:T(8,128)(2,1)} fusion(bf16[2,1024,512]{2,1,0:T(8,128)(2,1)} %copy.97, s32[256]{0:T(256)S(1)} %bitcast.167, bf16[256,512]{1,0:T(8,128)(2,1)S(1)} %copy.41), kind=kCustom, calls=%fused_computation.1 | custom fusion | bytes 788480 | tf_op jit(solution)/shard_map/scatter | solution.py:120
  123.6 6.8 %fusion.24 = bf16[4,128,256]{2,1,0:T(8,128)(2,1)S(1)} fusion(f32[4,2,1024,256]{3,2,1,0:T(8,128)} %copy-done.2, f32[256,4]{0,1:T(4,128)S(1)} %fusion.3, f32[256,4]{0,1:T(4,128)S(1)} %get-tuple-element.15, pred[256,2,1024]{0,2,1:T(8,128)(4,1)S(1)} %or_and_fusion, bf16[2,1024,512]{2,1,0:T(8,128)(2,1)} %scatter_fusion), kind=kOutput, calls=%fused_computation.38 | convolution fusion | flops 547487744 | bytes 11280384 | tf_op jit(solution)/shard_map/thrj,rjhd->thd/dot_general | solution.py:63
  130.4 1.7 convolution_convert_fusion.1
  132.1 0.0 reduce-scatter.2.cloned.1.call-update
  132.1 0.2 all-gather.5.cloned.1.call-start
  132.4 5.9 %copy.51 = bf16[2,3,2048,256]{3,2,0,1:T(8,128)(2,1)} copy(bf16[2,3,2048,256]{3,2,1,0:T(8,128)(2,1)} %param.25) | data formatting | bytes 12582912 | tf_op args[12]
  138.3 0.0 all-gather.5.cloned.1.call-update
  138.3 0.7 copy-done.7
  139.0 0.1 copy.48
  139.1 0.1 eq.88
  139.1 0.1 reshape.303
  139.3 1.2 reduce-window.16
  140.5 0.2 slice_reduce_fusion
  140.7 0.1 fusion.43
  140.9 16.6 %reduce-scatter.2.cloned.1.call-done = bf16[64,2048]{1,0:T(8,128)(2,1)} async-done(((bf16[256,2048]{1,0:T(8,128)(2,1)}), bf16[64,2048]{1,0:T(8,128)(2,1)}) %reduce-scatter.2.cloned.1.call-update) | async-done | bytes 262160 | tf_op jit(solution)/shard_map/reduce_scatter | solution.py:130
  157.5 1.2 fusion.35
  158.6 1.1 fusion.37
  159.7 2.3 convolution_convert_fusion
  162.0 59.6 %all_to_all.10 = bf16[32,2,16,2048]{3,2,1,0:T(8,128)(2,1)} all-to-all(bf16[32,2,16,2048]{3,2,1,0:T(8,128)(2,1)S(1)} %bitcast.169), channel_id=1, replica_groups=mesh['head'=4,'tok'=32] {'tok'}, dimensions={0} | all-to-all | bytes 8388608 | tf_op jit(solution)/shard_map/all_to_all | solution.py:155
  221.6 164.7 %all-gather.5.cloned.1.call-done = bf16[2,3,2048,1024]{3,2,0,1:T(8,128)(2,1)} async-done(((bf16[2,3,2048,256]{3,2,0,1:T(8,128)(2,1)}), bf16[2,3,2048,1024]{3,2,0,1:T(8,128)(2,1)}) %all-gather.5.cloned.1.call-update) | async-done | bytes 25165840 | tf_op jit(solution)/shard_map/all_gather | solution.py:156
  386.3 8.3 %fusion.1 = f32[2,32,16,1024]{3,2,1,0:T(8,128)S(1)} fusion(bf16[2,3,2048,1024]{3,2,0,1:T(8,128)(2,1)} %all-gather.5.cloned.1.call-done, bf16[32,2,16,2048]{3,2,1,0:T(8,128)(2,1)} %all_to_all.10), kind=kOutput, calls=%fused_computation.6 | convolution fusion | flops 4294967296 | bytes 16777216 | tf_op jit(solution)/shard_map/semd,edf->semf/dot_general | solution.py:72
  394.6 8.4 %fusion.6 = bf16[32,2,16,1024]{3,2,0,1:T(8,128)(2,1)S(1)} fusion(f32[2,32,16,1024]{3,2,1,0:T(8,128)S(1)} %fusion.1, bf16[2,3,2048,1024]{3,2,0,1:T(8,128)(2,1)} %all-gather.5.cloned.1.call-done, bf16[32,2,16,2048]{3,2,1,0:T(8,128)(2,1)S(1)} %copy-done.4), kind=kOutput, calls=%fused_computation.17 | convolution fusion | flops 4301258752 | bytes 18874368 | tf_op jit(solution)/shard_map/semd,edf->semf/dot_general | solution.py:69
  403.0 8.2 %convert_bitcast_fusion = bf16[32,2,16,2048]{3,2,0,1:T(8,128)(2,1)S(1)} fusion(bf16[32,2,16,1024]{3,2,0,1:T(8,128)(2,1)S(1)} %fusion.6, bf16[2,3,2048,1024]{3,2,0,1:T(8,128)(2,1)} %all-gather.5.cloned.1.call-done), kind=kOutput, calls=%fused_computation.23 | convolution fusion | flops 4297064448 | bytes 14680064 | tf_op jit(solution)/shard_map/semf,edf->semd/dot_general | solution.py:76
  411.2 2.3 copy.54
  413.5 9.2 %all-to-all-start.1 = ((bf16[32,2,16,2048]{3,2,1,0:T(8,128)(2,1)}), bf16[32,2,16,2048]{3,2,1,0:T(8,128)(2,1)}, u32[]{:S(2)}, u32[]{:S(2)}) async-start(bf16[32,2,16,2048]{3,2,1,0:T(8,128)(2,1)} %copy.54), calls=%async_computation.2 | async-start | bytes 8388608 | tf_op jit(solution)/shard_map/all_to_all | solution.py:159
  422.7 0.1 copy.55
  422.8 0.1 mul.209
  422.9 0.1 copy.47
  423.0 51.8 %all-to-all-done.1 = bf16[32,2,16,2048]{3,2,1,0:T(8,128)(2,1)} async-done(((bf16[32,2,16,2048]{3,2,1,0:T(8,128)(2,1)}), bf16[32,2,16,2048]{3,2,1,0:T(8,128)(2,1)}, u32[]{:S(2)}, u32[]{:S(2)}) %all-to-all-start.1) | async-done | bytes 4194336 | tf_op jit(solution)/shard_map/all_to_all | solution.py:159
  474.8 8.1 %gather_fusion = bf16[512,2048]{1,0:T(8,128)(2,1)} fusion(bf16[1024,2048]{1,0:T(8,128)(2,1)} %bitcast.36, s32[1024]{0:T(1024)S(1)} %pad_clamp_fusion), kind=kCustom, calls=%fused_computation | custom fusion | bytes 4196352 | tf_op jit(solution)/shard_map/gather | solution.py:160
  483.0 3.4 fusion.5
  486.4 0.8 fusion.38
  (44 shorter events, 0.2 us)
Async XLA Ops:
  7.2 123.2 %copy-start = (bf16[512,2048]{1,0:T(8,128)(2,1)S(1)}, bf16[512,2048]{1,0:T(8,128)(2,1)}, u32[]{:S(2)}) copy-start(bf16[512,2048]{1,0:T(8,128)(2,1)} %param.21) | copy-start | bytes 6291460
  7.2 5.7 %copy-start.14 = (u32[128]{0:T(128)S(1)}, u32[128]{0:T(128)}, u32[]{:S(2)}) copy-start(u32[128]{0:T(128)} %constant.89) | copy-start | bytes 1540
  7.2 4.6 copy-start.3
  7.2 7.1 %copy-start.13 = (s32[64]{0:T(128)S(1)}, s32[64]{0:T(128)}, u32[]{:S(2)}) copy-start(s32[64]{0:T(128)} %param.14) | copy-start | bytes 772
  7.2 4.8 copy-start.8
  7.2 31.0 %all-gather.3.cloned.1.call-start = ((), (), s32[]{:S(2)}) async-start(), calls=%async_computation.3 | async-start | bytes 1310720 | tf_op jit(solution)/shard_map/all_gather | solution.py:101
  7.3 3.2 copy-start.6
  12.8 144.6 %reduce-scatter.2.cloned.1.call-start = ((), (), s32[]{:S(2)}) async-start(), calls=%async_computation.4 | async-start | bytes 1310720 | tf_op jit(solution)/shard_map/reduce_scatter | solution.py:130
  23.5 8.9 %copy-start.11 = (s32[2]{0:T(128)S(1)}, s32[2]{0:T(128)}, u32[]{:S(2)}) copy-start(s32[2]{0:T(128)} %param.15) | copy-start | bytes 28
  23.5 9.0 %copy-start.12 = (s32[2]{0:T(128)S(1)}, s32[2]{0:T(128)}, u32[]{:S(2)}) copy-start(s32[2]{0:T(128)} %param.16) | copy-start | bytes 28
  84.0 3.2 copy-start.2
  132.1 254.2 %all-gather.5.cloned.1.call-start = ((), (), s32[]{:S(2)}) async-start(), calls=%async_computation.5 | async-start | bytes 31457280 | tf_op jit(solution)/shard_map/all_gather | solution.py:156
  138.3 0.7 copy-start.7
  138.3 20.4 %copy-start.9 = (f32[2048]{0:T(1024)S(1)}, f32[2048]{0:T(1024)}, u32[]{:S(2)}) copy-start(f32[2048]{0:T(1024)} %param.22) | copy-start | bytes 24580
  386.3 8.3 %copy-start.4 = (bf16[32,2,16,2048]{3,2,1,0:T(8,128)(2,1)S(1)}, bf16[32,2,16,2048]{3,2,1,0:T(8,128)(2,1)}, u32[]{:S(2)}) copy-start(bf16[32,2,16,2048]{3,2,1,0:T(8,128)(2,1)} %all_to_all.10) | copy-start | bytes 12582916
  413.5 9.4 %copy-start.10 = (f32[64,8]{0,1:T(8,128)S(1)}, f32[64,8]{0,1:T(8,128)}, u32[]{:S(2)}) copy-start(f32[64,8]{0,1:T(8,128)} %param.24) | copy-start | bytes 6148
  413.5 61.3 %all-to-all-start.1 = ((bf16[32,2,16,2048]{3,2,1,0:T(8,128)(2,1)}), bf16[32,2,16,2048]{3,2,1,0:T(8,128)(2,1)}, u32[]{:S(2)}, u32[]{:S(2)}) async-start(bf16[32,2,16,2048]{3,2,1,0:T(8,128)(2,1)} %copy.54), calls=%async_computation.2 | async-start | bytes 8388608 | tf_op jit(solution)/shard_map/all_to_all | solution.py:159
  474.8 11.6 %copy-start.5 = (bf16[64,2048]{1,0:T(8,128)(2,1)S(1)}, bf16[64,2048]{1,0:T(8,128)(2,1)}, u32[]{:S(2)}) copy-start(bf16[64,2048]{1,0:T(8,128)(2,1)} %reduce-scatter.2.cloned.1.call-done) | copy-start | bytes 786436
  474.8 12.4 %copy-start.1 = (bf16[512,2048]{1,0:T(8,128)(2,1)S(1)}, bf16[512,2048]{1,0:T(8,128)(2,1)}, u32[]{:S(2)}) copy-start(bf16[512,2048]{1,0:T(8,128)(2,1)} %param.21) | copy-start | bytes 6291460
Sparse Core Ops, SparseCore 0:
  13.0 25.2 all-gather.2
  132.3 25.1 reduce-scatter.1
  159.1 227.1 all-gather.4
where the time goes:
time: 496 us; the launch traced here: 494 us
  waiting for transfers between devices  238 us (48%)
  local copies, waits for them, and re-layouts  107 us (22%)
  blocking collectives  67.4 us (14%)
  matrix products  43.7 us (9%)
  between operations  14.8 us (3%)
  other arithmetic  13.7 us (3%)
  starting transfers between devices  9.53 us (2%)
    all_gather x1, waiting for transfers between devices, on_device(): lax.all_gather(w_expert, 'head', axis=3, tiled=True)  165 us
    all_to_all x1, blocking collectives, on_device(): lax.all_to_all(outgoing, 'tok', split_axis=0, concat_axis=0, tiled=True)  59.6 us
    all_to_all x1, waiting for transfers between devices, on_device(): lax.all_to_all(result, 'tok', split_axis=0, concat_axis=0, tiled=True)  51.8 us
    scatter x1, local copies, waits for them, and re-layouts, on_device(): cache_keys = cache_k.at[group_req, positions_all].set(key_new)  34.8 us
    scatter x1, local copies, waits for them, and re-layouts, on_device(): cache_values = cache_v.at[group_req, positions_all].set(value_new)  34.6 us
    unnamed x39, local copies, waits for them, and re-layouts  24.3 us
    reduce_scatter x1, waiting for transfers between devices, on_device(): lax.psum_scatter(jnp.dot(attended, w_out, preferred_element_type=jnp.floa...  16.6 us
  transfers between devices with their start and end apart: 4, of which 4 were waited for; matrix products, arithmetic and copies ran while one was open for 5% of the time, Pallas kernels for 0%

commit v1 on v0

--- a/solution.py
+++ b/solution.py
@@ -153,9 +153,12 @@
     outgoing = jnp.dot(dispatch, repeated, preferred_element_type=jnp.float32).astype(jnp.bfloat16)
     outgoing = outgoing.reshape(tok_count, exp_dev, slot_depth, model_width)
     arrived = lax.all_to_all(outgoing, "tok", split_axis=0, concat_axis=0, tiled=True)
-    result = expert_apply(arrived, lax.all_gather(w_expert, "head", axis=3, tiled=True)).astype(
-        jnp.bfloat16
-    )
+    result = expert_apply(
+        arrived,
+        jnp.concatenate(
+            lax.all_to_all(jnp.stack([w_expert] * lax.axis_size("head")), "head", 0, 0), axis=3
+        ),
+    ).astype(jnp.bfloat16)
     returned = lax.all_to_all(result, "tok", split_axis=0, concat_axis=0, tiled=True)
     picked = returned.reshape(-1, model_width)[target].reshape(tok_dev, route_count, model_width)
     combined = jnp.sum(route_weight[:, :, None] * picked.astype(jnp.float32), axis=1)

time: 496 us -> 616 us (1.24)
  blocking collectives: 67.4 us -> 282 us
  waiting for transfers between devices: 238 us -> 105 us
  local copies, waits for them, and re-layouts: 107 us -> 129 us
  starting transfers between devices: 9.53 us -> 25.1 us
    unnamed x1, blocking collectives: 7.85 us -> 282 us
    all_gather x1 -> x0, waiting for transfers between devices: 165 us -> none  [on_device(): lax.all_gather(w_expert, 'head', axis=3, tiled=True)]
    all_to_all x1 -> x0, blocking collectives: 59.6 us -> none  [on_device(): lax.all_to_all(outgoing, 'tok', split_axis=0, concat_axis=0, tiled=True)]
    all_to_all x0 -> x2, waiting for transfers between devices: none -> 30.9 us  [the longest x1 30.9 us: on_device(): lax.all_to_all(outgoing, 'tok', split_axis=0, concat_axis=0, tiled=True)]
    reshape x0 -> x1, local copies, waits for them, and re-layouts: none -> 21.2 us  [on_device(): jnp.concatenate(lax.all_to_all(jnp.stack([w_expert] * lax.axis_size('head...]
    all_to_all x0 -> x2, starting transfers between devices: none -> 17.8 us  [the longest x1 9.27 us: on_device(): lax.all_to_all(outgoing, 'tok', split_axis=0, concat_axis=0, tiled=True)]
    another operation x2 -> x3, local copies, waits for them, and re-layouts: 0.24 us -> 8.79 us  [the longest x1 8.56 us: on_device(): jnp.stack([w_expert] * lax.axis_size('head'))]
    unnamed x39 -> x41, local copies, waits for them, and re-layouts: 24.3 us -> 16 us
  transfers between devices with their start and end apart: 4 -> 5, of which waited for: 4 -> 3; matrix products, arithmetic and copies ran while one was open for 5% -> 21% of each run, Pallas kernels for 0% -> 0%
where the time goes in v1:
time: 616 us; the launch traced here: 613 us
  blocking collectives  282 us (46%)
  local copies, waits for them, and re-layouts  129 us (21%)
  waiting for transfers between devices  105 us (17%)
  matrix products  43 us (7%)
  starting transfers between devices  25.1 us (4%)
  between operations  15 us (2%)
  other arithmetic  13.9 us (2%)
    unnamed x1, blocking collectives  282 us
    all_to_all x1, waiting for transfers between devices, on_device(): lax.all_to_all(result, 'tok', split_axis=0, concat_axis=0, tiled=True)  51.8 us
    scatter x1, local copies, waits for them, and re-layouts, on_device(): cache_keys = cache_k.at[group_req, positions_all].set(key_new)  34.9 us
    scatter x1, local copies, waits for them, and re-layouts, on_device(): cache_values = cache_v.at[group_req, positions_all].set(value_new)  34.8 us
    all_to_all x1, waiting for transfers between devices, on_device(): lax.all_to_all(outgoing, 'tok', split_axis=0, concat_axis=0, tiled=True)  30.9 us
    reduce_scatter x1, waiting for transfers between devices, on_device(): lax.psum_scatter(jnp.dot(attended, w_out, preferred_element_type=jnp.floa...  22.5 us
    reshape x1, local copies, waits for them, and re-layouts, on_device(): jnp.concatenate(lax.all_to_all(jnp.stack([w_expert] * lax.axis_size('head...  21.2 us
    unnamed x41, local copies, waits for them, and re-layouts  16 us
  transfers between devices with their start and end apart: 5, of which 3 were waited for; matrix products, arithmetic and copies ran while one was open for 21% of the time, Pallas kernels for 0%

profile of v1, /device:TPU:1, one launch (start us, length us, event | category | flops | bytes accessed | tf_op | source)
XLA Modules:
  0.0 612.9 jit_solution(9315797034348951782)
XLA Ops:
  7.2 0.0 copy-start
  7.2 3.2 copy.98
  10.4 1.3 copy.99
  11.7 1.2 copy-done.4
  12.9 0.4 copy.51
  13.3 8.6 %stack.2 = bf16[4,2,3,2048,256]{4,3,1,2,0:T(8,128)(2,1)} broadcast(bf16[2,3,2048,256]{3,2,0,1:T(8,128)(2,1)S(1)} %copy.51), dimensions={1,2,3,4} | broadcast | bytes 31457280 | tf_op jit(solution)/shard_map/stack | solution.py:159
  21.9 8.6 %all-to-all-start.1 = ((bf16[4,2,3,2048,256]{4,3,1,2,0:T(8,128)(2,1)}), bf16[4,2,3,2048,256]{4,3,1,2,0:T(8,128)(2,1)}, u32[]{:S(2)}, u32[]{:S(2)}) async-start(bf16[4,2,3,2048,256]{4,3,1,2,0:T(8,128)(2,1)} %stack.2), calls=%async_computation.2 | async-start | bytes 50331648 | tf_op jit(solution)/shard_map/all_to_all | solution.py:159
  30.4 0.0 all-gather.2.cloned.1.call-start
  30.5 0.2 fusion.31
  30.7 0.8 fusion.33
  31.5 0.0 all-gather.2.cloned.1.call-update
  31.5 0.0 reduce-scatter.2.cloned.1.call-start
  31.6 0.6 dynamic-slice
  32.8 0.2 dynamic-update-slice
  33.1 281.7 %all-reduce = s32[256]{0:T(256)S(1)} all-reduce(s32[256]{0:T(256)S(1)} %dynamic-update-slice), channel_id=1, replica_groups=mesh['head'=4,'tok'=32] {'head'}, use_global_device_ids=true, to_apply=%add | all-reduce | flops 256 | bytes 2048
  314.8 0.6 reduce-window.14
  315.4 0.2 slice_reduce_fusion.1
  315.6 0.2 reduce-window.15
  315.8 0.1 add_bitcast_fusion.1
  315.9 8.8 %copy.40 = bf16[2048,3,512]{0,2,1:T(8,128)(2,1)} copy(bf16[2048,3,512]{2,0,1:T(8,128)(2,1)} %param.20) | data formatting | bytes 12582912 | tf_op args[7]
  324.8 0.1 fusion.48
  324.9 0.1 iota_compare_fusion.6
  325.0 0.3 multiply_cosine_fusion
  325.3 0.3 iota_compare_fusion.2
  325.6 0.6 or_and_fusion
  326.2 0.0 all-gather.2.cloned.1.call-done
  326.2 5.0 fusion.27
  331.2 0.7 slice.98
  332.0 0.1 slice_bitcast_fusion.10
  332.1 0.8 subtract_convert_fusion
  332.9 0.1 copy.42
  333.0 1.1 copy.41
  334.1 34.9 %scatter_fusion.1 = bf16[2,1024,512]{2,1,0:T(8,128)(2,1)} fusion(bf16[2,1024,512]{2,1,0:T(8,128)(2,1)} %copy.98, s32[256]{0:T(256)S(1)} %bitcast.169, bf16[256,512]{1,0:T(8,128)(2,1)S(1)} %copy.42), kind=kCustom, calls=%fused_computation.2 | custom fusion | bytes 788480 | tf_op jit(solution)/shard_map/scatter | solution.py:119
  369.0 34.8 %scatter_fusion = bf16[2,1024,512]{2,1,0:T(8,128)(2,1)} fusion(bf16[2,1024,512]{2,1,0:T(8,128)(2,1)} %copy.99, s32[256]{0:T(256)S(1)} %bitcast.170, bf16[256,512]{1,0:T(8,128)(2,1)S(1)} %copy.41), kind=kCustom, calls=%fused_computation.1 | custom fusion | bytes 788480 | tf_op jit(solution)/shard_map/scatter | solution.py:120
  403.8 3.1 fusion.4
  406.9 1.8 fusion.3
  408.7 2.9 fusion.24
  411.6 1.7 convolution_convert_fusion.1
  413.3 0.0 reduce-scatter.2.cloned.1.call-update
  413.4 0.1 copy.48
  413.5 0.1 reshape.311
  413.5 0.1 eq.88
  413.7 1.4 reduce-window.16
  415.0 0.2 slice_reduce_fusion
  415.3 0.1 fusion.43
  415.4 22.5 %reduce-scatter.2.cloned.1.call-done = bf16[64,2048]{1,0:T(8,128)(2,1)} async-done(((bf16[256,2048]{1,0:T(8,128)(2,1)}), bf16[64,2048]{1,0:T(8,128)(2,1)}) %reduce-scatter.2.cloned.1.call-update) | async-done | bytes 262160 | tf_op jit(solution)/shard_map/reduce_scatter | solution.py:130
  438.0 1.2 fusion.35
  439.2 1.1 fusion.37
  440.2 4.4 convolution_convert_fusion
  444.6 9.3 %all-to-all-start = ((bf16[32,2,16,2048]{3,2,1,0:T(8,128)(2,1)}), bf16[32,2,16,2048]{3,2,1,0:T(8,128)(2,1)}, u32[]{:S(2)}, u32[]{:S(2)}) async-start(bf16[32,2,16,2048]{3,2,1,0:T(8,128)(2,1)} %bitcast.175), calls=%async_computation.1 | async-start | bytes 8388608 | tf_op jit(solution)/shard_map/all_to_all | solution.py:155
  453.9 21.2 %copy.69 = bf16[4,3,2,256,8,256]{5,4,0,3,2,1:T(8,128)(2,1)} copy(bf16[4,3,2,256,8,256]{5,4,3,2,1,0:T(8,128)(2,1)} %bitcast.57) | data formatting | bytes 50331648 | tf_op jit(solution)/shard_map/reshape | solution.py:158
  475.1 30.9 %all-to-all-done = bf16[32,2,16,2048]{3,2,1,0:T(8,128)(2,1)} async-done(((bf16[32,2,16,2048]{3,2,1,0:T(8,128)(2,1)}), bf16[32,2,16,2048]{3,2,1,0:T(8,128)(2,1)}, u32[]{:S(2)}, u32[]{:S(2)}) %all-to-all-start) | async-done | bytes 4194336 | tf_op jit(solution)/shard_map/all_to_all | solution.py:155
  506.0 8.1 %fusion.1 = f32[2,32,16,1024]{3,2,1,0:T(8,128)S(1)} fusion(bf16[2,3,2048,1024]{3,2,0,1:T(8,128)(2,1)} %bitcast.171, bf16[32,2,16,2048]{3,2,1,0:T(8,128)(2,1)} %all-to-all-done), kind=kOutput, calls=%fused_computation.6 | convolution fusion | flops 4294967296 | bytes 16777216 | tf_op jit(solution)/shard_map/semd,edf->semf/dot_general | solution.py:72
  514.1 9.7 %fusion.6 = bf16[32,2,16,1024]{3,2,0,1:T(8,128)(2,1)S(1)} fusion(f32[2,32,16,1024]{3,2,1,0:T(8,128)S(1)} %fusion.1, bf16[2,3,2048,1024]{3,2,0,1:T(8,128)(2,1)} %bitcast.172, bf16[32,2,16,2048]{3,2,1,0:T(8,128)(2,1)} %all-to-all-done), kind=kOutput, calls=%fused_computation.17 | convolution fusion | flops 4301258752 | bytes 18874368 | tf_op jit(solution)/shard_map/semd,edf->semf/dot_general | solution.py:69
  523.8 8.2 %convert_bitcast_fusion = bf16[32,2,16,2048]{3,2,0,1:T(8,128)(2,1)S(1)} fusion(bf16[32,2,16,1024]{3,2,0,1:T(8,128)(2,1)S(1)} %fusion.6, bf16[2,3,2048,1024]{3,2,0,1:T(8,128)(2,1)} %bitcast.173), kind=kOutput, calls=%fused_computation.23 | convolution fusion | flops 4297064448 | bytes 14680064 | tf_op jit(solution)/shard_map/semf,edf->semd/dot_general | solution.py:76
  532.0 2.3 copy.55
  534.3 7.2 %all-to-all-start.2 = ((bf16[32,2,16,2048]{3,2,1,0:T(8,128)(2,1)}), bf16[32,2,16,2048]{3,2,1,0:T(8,128)(2,1)}, u32[]{:S(2)}, u32[]{:S(2)}) async-start(bf16[32,2,16,2048]{3,2,1,0:T(8,128)(2,1)} %copy.55), calls=%async_computation.3 | async-start | bytes 8388608 | tf_op jit(solution)/shard_map/all_to_all | solution.py:162
  541.5 0.1 copy.56
  541.6 0.1 mul.209
  541.7 0.1 copy.47
  541.8 51.8 %all-to-all-done.2 = bf16[32,2,16,2048]{3,2,1,0:T(8,128)(2,1)} async-done(((bf16[32,2,16,2048]{3,2,1,0:T(8,128)(2,1)}), bf16[32,2,16,2048]{3,2,1,0:T(8,128)(2,1)}, u32[]{:S(2)}, u32[]{:S(2)}) %all-to-all-start.2) | async-done | bytes 4194336 | tf_op jit(solution)/shard_map/all_to_all | solution.py:162
  593.6 8.1 %gather_fusion = bf16[512,2048]{1,0:T(8,128)(2,1)} fusion(bf16[1024,2048]{1,0:T(8,128)(2,1)} %bitcast.37, s32[1024]{0:T(1024)S(1)} %pad_clamp_fusion), kind=kCustom, calls=%fused_computation | custom fusion | bytes 4196352 | tf_op jit(solution)/shard_map/gather | solution.py:163
  601.8 3.4 fusion.5
  605.2 0.8 fusion.38
  (48 shorter events, 0.2 us)
Async XLA Ops:
  7.2 404.4 %copy-start = (bf16[512,2048]{1,0:T(8,128)(2,1)S(1)}, bf16[512,2048]{1,0:T(8,128)(2,1)}, u32[]{:S(2)}) copy-start(bf16[512,2048]{1,0:T(8,128)(2,1)} %param.21) | copy-start | bytes 6291460
  7.2 3.2 copy-start.6
  7.2 5.7 copy-start.4
  21.9 8.6 %copy-start.3 = (bf16[64,2048]{1,0:T(8,128)(2,1)S(1)}, bf16[64,2048]{1,0:T(8,128)(2,1)}, u32[]{:S(2)}) copy-start(bf16[64,2048]{1,0:T(8,128)(2,1)} %param.13) | copy-start | bytes 786436
  21.9 8.8 %copy-start.9 = (f32[2048]{0:T(1024)S(1)}, f32[2048]{0:T(1024)}, u32[]{:S(2)}) copy-start(f32[2048]{0:T(1024)} %param.19) | copy-start | bytes 24580
  21.9 9.7 %copy-start.15 = (u32[128]{0:T(128)S(1)}, u32[128]{0:T(128)}, u32[]{:S(2)}) copy-start(u32[128]{0:T(128)} %constant.89) | copy-start | bytes 1540
  21.9 11.0 %copy-start.14 = (s32[64]{0:T(128)S(1)}, s32[64]{0:T(128)}, u32[]{:S(2)}) copy-start(s32[64]{0:T(128)} %param.14) | copy-start | bytes 772
  21.9 422.7 %all-to-all-start.1 = ((bf16[4,2,3,2048,256]{4,3,1,2,0:T(8,128)(2,1)}), bf16[4,2,3,2048,256]{4,3,1,2,0:T(8,128)(2,1)}, u32[]{:S(2)}, u32[]{:S(2)}) async-start(bf16[4,2,3,2048,256]{4,3,1,2,0:T(8,128)(2,1)} %stack.2), calls=%async_computation.2 | async-start | bytes 50331648 | tf_op jit(solution)/shard_map/all_to_all | solution.py:159
  30.4 295.7 %all-gather.2.cloned.1.call-start = ((), (), s32[]{:S(2)}) async-start(), calls=%async_computation.4 | async-start | bytes 1310720 | tf_op jit(solution)/shard_map/all_gather | solution.py:101
  31.5 406.4 %reduce-scatter.2.cloned.1.call-start = ((), (), s32[]{:S(2)}) async-start(), calls=%async_computation.5 | async-start | bytes 1310720 | tf_op jit(solution)/shard_map/reduce_scatter | solution.py:130
  315.9 8.9 %copy-start.12 = (s32[2]{0:T(128)S(1)}, s32[2]{0:T(128)}, u32[]{:S(2)}) copy-start(s32[2]{0:T(128)} %param.15) | copy-start | bytes 28
  315.9 9.0 %copy-start.13 = (s32[2]{0:T(128)S(1)}, s32[2]{0:T(128)}, u32[]{:S(2)}) copy-start(s32[2]{0:T(128)} %param.16) | copy-start | bytes 28
  369.0 34.8 %copy-start.7 = (bf16[256,4,64]{0,2,1:T(8,128)(2,1)S(1)}, bf16[256,4,64]{0,2,1:T(8,128)(2,1)}, u32[]{:S(2)}) copy-start(bf16[256,4,64]{0,2,1:T(8,128)(2,1)} %get-tuple-element.6) | copy-start | bytes 393220
  406.8 1.9 copy-start.2
  411.6 1.8 copy-start.8
  411.6 27.6 %copy-start.10 = (f32[2048]{0:T(1024)S(1)}, f32[2048]{0:T(1024)}, u32[]{:S(2)}) copy-start(f32[2048]{0:T(1024)} %param.22) | copy-start | bytes 24580
  444.6 61.4 %all-to-all-start = ((bf16[32,2,16,2048]{3,2,1,0:T(8,128)(2,1)}), bf16[32,2,16,2048]{3,2,1,0:T(8,128)(2,1)}, u32[]{:S(2)}, u32[]{:S(2)}) async-start(bf16[32,2,16,2048]{3,2,1,0:T(8,128)(2,1)} %bitcast.175), calls=%async_computation.1 | async-start | bytes 8388608 | tf_op jit(solution)/shard_map/all_to_all | solution.py:155
  534.3 7.4 %copy-start.11 = (f32[64,8]{0,1:T(8,128)S(1)}, f32[64,8]{0,1:T(8,128)}, u32[]{:S(2)}) copy-start(f32[64,8]{0,1:T(8,128)} %param.24) | copy-start | bytes 6148
  534.3 59.3 %all-to-all-start.2 = ((bf16[32,2,16,2048]{3,2,1,0:T(8,128)(2,1)}), bf16[32,2,16,2048]{3,2,1,0:T(8,128)(2,1)}, u32[]{:S(2)}, u32[]{:S(2)}) async-start(bf16[32,2,16,2048]{3,2,1,0:T(8,128)(2,1)} %copy.55), calls=%async_computation.3 | async-start | bytes 8388608 | tf_op jit(solution)/shard_map/all_to_all | solution.py:162
  593.6 11.6 %copy-start.5 = (bf16[64,2048]{1,0:T(8,128)(2,1)S(1)}, bf16[64,2048]{1,0:T(8,128)(2,1)}, u32[]{:S(2)}) copy-start(bf16[64,2048]{1,0:T(8,128)(2,1)} %reduce-scatter.2.cloned.1.call-done) | copy-start | bytes 786436
  593.6 12.4 %copy-start.1 = (bf16[512,2048]{1,0:T(8,128)(2,1)S(1)}, bf16[512,2048]{1,0:T(8,128)(2,1)}, u32[]{:S(2)}) copy-start(bf16[512,2048]{1,0:T(8,128)(2,1)} %param.21) | copy-start | bytes 6291460
Sparse Core Ops, SparseCore 0:
  33.5 34.1 all-gather.1
  413.5 24.4 reduce-scatter.1
